TPU v7x, 32 devices: a whole 2x2x4 slice. The times are simulated.
32 devices in a mesh: groups: 2 (over x), ctx: 16 (over z, y, core).
Axes of the slice: x: 2, y: 2, z: 4, core: 2. Of those that a mesh axis runs over, the one named last changes fastest.
Arguments:
- context_keys: bfloat16 [4096, 2048], P(('groups', 'ctx')), parts along dimension 0, may hold values from -6 to 6
- context_values: bfloat16 [4096, 2048], P(('groups', 'ctx')), parts along dimension 0, may hold values from -6 to 6
- context_queries: bfloat16 [4096, 2048], P(('groups', 'ctx')), parts along dimension 0, may hold values from -6 to 6
- token_rates: float32 [8, 4096], P(None, ('groups', 'ctx')), parts along dimension 1, may hold values from 0.05 to 1
- w_gate: bfloat16 [8, 256, 256], replicated, may hold values from -0.375 to 0.375
- w_up: bfloat16 [8, 256, 256], replicated, may hold values from -0.375 to 0.375
- w_down: bfloat16 [8, 256, 256], replicated, may hold values from -0.375 to 0.375
- question_rows: bfloat16 [8192, 2048], P(('groups', 'ctx')), parts along dimension 0, may hold values from -6 to 6
- question_count: int32 [32], P(('groups', 'ctx')), parts along dimension 0, may hold values from 1 to 256, 1024 in all
Outputs:
- context_out: bfloat16 [4096, 2048], P(('groups', 'ctx')), parts along dimension 0
- answers: bfloat16 [8192, 2048], P(('groups', 'ctx')), parts along dimension 0
There are 2 independent parts, one for each index of `groups`. A program takes and returns all parts, laid end to end along the dimension named above; an argument that names none is the same for every part. Nothing has to cross between parts.
Inputs may be any that keep to these rules, and one draw needn't show every extreme that they name: `question_count`: live rows are the first of each device's 256 slots. The counts of one user (the devices along ctx) add up to exactly 1024, and some device of each user has exactly 256.
All inputs are finite; a program needn't handle non-finite values.
Results may differ from a plain program's by a relative error of at most 0.018.
Values may be sent and summed in bfloat16 or wider, within the bound.
A program may use at most 128 MiB of HBM per device.

v0:
```python
import jax
import jax.numpy as jnp
from jax import lax
from jax.sharding import PartitionSpec as P

NS_STEPS = 3
quintic_first = 3.4445
quintic_second = -4.775
quintic_third = 2.0315


def fast_apply(in_rows, w_gate, w_up, w_down):
    head_count = w_gate.shape[0]
    head_size = w_gate.shape[1]
    row_split = in_rows.reshape(in_rows.shape[0], head_count, head_size)
    pre_gate = jnp.einsum("thd,hde->hte", row_split, w_gate, preferred_element_type=jnp.float32)
    pre_up = jnp.einsum("thd,hde->hte", row_split, w_up, preferred_element_type=jnp.float32)
    hidden = (jax.nn.silu(pre_gate) * pre_up).astype(jnp.bfloat16)
    outputs = jnp.einsum("hte,hef->thf", hidden, w_down, preferred_element_type=jnp.float32)
    return outputs.reshape(in_rows.shape[0], head_count * head_size).astype(jnp.bfloat16)


def directions(context_keys, context_values, token_rates, w_gate, w_up, w_down):
    tok_rows = context_keys.shape[0]
    head_count = w_gate.shape[0]
    head_size = w_gate.shape[1]
    key_split = context_keys.reshape(tok_rows, head_count, head_size)
    value_split = context_values.reshape(tok_rows, head_count, head_size)
    pre_gate = jnp.einsum("thd,hde->hte", key_split, w_gate, preferred_element_type=jnp.float32)
    pre_up = jnp.einsum("thd,hde->hte", key_split, w_up, preferred_element_type=jnp.float32)
    sigmoid_gate = jax.nn.sigmoid(pre_gate)
    activated = pre_gate * sigmoid_gate
    hidden = (activated * pre_up).astype(jnp.bfloat16)
    weighted = (token_rates.T[:, :, None] * value_split).astype(jnp.bfloat16)
    back_hidden = jnp.einsum("thf,hef->hte", weighted, w_down, preferred_element_type=jnp.float32)
    back_gate = (
        back_hidden * pre_up * sigmoid_gate * (1.0 + pre_gate * (1.0 - sigmoid_gate))
    ).astype(jnp.bfloat16)
    back_up = (back_hidden * activated).astype(jnp.bfloat16)
    step_gate = jnp.einsum("thd,hte->hde", key_split, back_gate, preferred_element_type=jnp.float32)
    step_up = jnp.einsum("thd,hte->hde", key_split, back_up, preferred_element_type=jnp.float32)
    step_down = jnp.einsum("hte,thf->hef", hidden, weighted, preferred_element_type=jnp.float32)
    return jnp.stack([step_gate, step_up, step_down])


def per_device(
    context_keys,
    context_values,
    context_queries,
    token_rates,
    w_gate,
    w_up,
    w_down,
    question_rows,
    question_count,
):
    head_count = w_gate.shape[0]
    head_size = w_gate.shape[1]
    matrix_count = 3 * head_count
    context_out = fast_apply(context_queries, w_gate, w_up, w_down)
    direction = directions(context_keys, context_values, token_rates, w_gate, w_up, w_down)
    flat_grads = direction.reshape(matrix_count, head_size * head_size)
    total = lax.psum(flat_grads, "ctx")
    norm_sizes = jnp.sqrt(jnp.sum(total * total, axis=1, keepdims=True))
    scaled = (total / (norm_sizes + 1e-06)).astype(jnp.bfloat16)
    iterate = scaled.reshape(matrix_count, head_size, head_size)
    for sweep_index in range(NS_STEPS):
        gram_matrix = jnp.einsum(
            "mij,mkj->mik", iterate, iterate, preferred_element_type=jnp.float32
        ).astype(jnp.bfloat16)
        gram_square = jnp.einsum(
            "mij,mjk->mik", gram_matrix, gram_matrix, preferred_element_type=jnp.float32
        )
        polynomial = (
            quintic_second * gram_matrix.astype(jnp.float32) + quintic_third * gram_square
        ).astype(jnp.bfloat16)
        product = jnp.einsum(
            "mij,mjk->mik", polynomial, iterate, preferred_element_type=jnp.float32
        )
        iterate = (quintic_first * iterate.astype(jnp.float32) + product).astype(jnp.bfloat16)
    previous = jnp.stack([w_gate, w_up, w_down]).astype(jnp.float32)
    moved = previous + iterate.reshape(3, head_count, head_size, head_size).astype(jnp.float32)
    col_norms = jnp.sqrt(jnp.sum(previous * previous, axis=2, keepdims=True))
    updated = (
        moved * col_norms / jnp.sqrt(jnp.sum(moved * moved, axis=2, keepdims=True) + 1e-06)
    ).astype(jnp.bfloat16)
    capacity = question_rows.shape[0]
    outputs = fast_apply(question_rows, updated[0], updated[1], updated[2])
    live_mask = jnp.arange(capacity, dtype=jnp.int32) < question_count[0]
    answers = jnp.where(live_mask[:, None], outputs, jnp.zeros_like(outputs))
    return (context_out, answers)


def solution(mesh):
    return jax.shard_map(
        per_device,
        mesh=mesh,
        in_specs=(
            P(("groups", "ctx"), None),
            P(("groups", "ctx"), None),
            P(("groups", "ctx"), None),
            P(None, ("groups", "ctx")),
            P(),
            P(),
            P(),
            P(("groups", "ctx"), None),
            P(("groups", "ctx")),
        ),
        out_specs=(P(("groups", "ctx"), None), P(("groups", "ctx"), None)),
        check_vma=False,
    )
```

profile of v0, /device:TPU:0, one launch (start us, length us, event | category | flops | bytes accessed | tf_op | source)
XLA Modules:
  0.0 236.1 jit_solution(8442899116746412055)
XLA Ops:
  7.2 0.0 copy-start.11
  7.2 0.0 all-reduce.2.cloned.1.call-start
  7.2 0.0 copy-start.9
  7.3 1.8 fusion.41
  9.1 1.4 fusion.43
  10.5 0.1 convert_element_type.148
  10.6 0.5 fusion.61
  11.1 0.0 copy-start.15
  11.1 0.7 convolution_bitcast_fusion
  11.8 0.4 copy-done.15
  12.1 0.6 convolution_bitcast_fusion.2
  12.8 0.6 convolution_bitcast_fusion.1
  13.4 3.3 %pad_maximum_fusion = f32[3,8,256,256]{2,3,1,0:T(8,128)} fusion(f32[1,8,256,256]{2,3,1,0:T(8,128)S(1)} %convolution_bitcast_fusion, f32[1,8,256,256]{2,3,1,0:T(8,128)S(1)} %convolution_bitcast_fusion.1, f32[1,8,256,256]{2,3,1,0:T(8,128)S(1)} %convolution_bitcast_fusion.2), kind=kLoop, calls=%fused_computation | loop fusion | flops 3145728 | bytes 12582912 | tf_op jit(solution)/shard_map/stack | solution.py:43
  16.7 6.7 %copy.60 = f32[3,8,256,256]{3,1,2,0:T(8,128)} copy(f32[3,8,256,256]{2,3,1,0:T(8,128)} %pad_maximum_fusion) | data formatting | bytes 12582912
  23.4 0.0 all-reduce.2.cloned.1.call-update
  23.4 1.2 copy-done.7
  24.6 0.5 copy.31
  25.1 0.5 copy.32
  25.7 1.9 copy.33
  27.5 3.1 %maximum_convert_fusion = f32[3,8,256,256]{2,3,1,0:T(8,128)} fusion(bf16[1,8,256,256]{2,3,1,0:T(8,128)(2,1)S(1)} %bitcast.124, bf16[1,8,256,256]{2,3,1,0:T(8,128)(2,1)S(1)} %bitcast.121, bf16[1,8,256,256]{2,3,1,0:T(8,128)(2,1)S(1)} %bitcast.118), kind=kLoop, calls=%fused_computation.18 | loop fusion | flops 4718592 | bytes 9437184 | tf_op jit(solution)/shard_map/convert_element_type | solution.py:81
  30.6 7.0 %copy.45 = f32[3,8,256,256]{3,2,1,0:T(8,128)} copy(f32[3,8,256,256]{2,3,1,0:T(8,128)} %maximum_convert_fusion) | data formatting | bytes 12582912 | tf_op jit(solution)/shard_map/convert_element_type | solution.py:81
  37.6 1.0 multiply_reduce_fusion
  38.6 0.0 copy-start.10
  38.6 0.0 copy-start.12
  38.6 2.4 %copy.56 = bf16[256,2048]{0,1:T(8,128)(2,1)} copy(bf16[256,2048]{1,0:T(8,128)(2,1)} %param.16) | data formatting | bytes 2097152 | tf_op jit(solution)/shard_map/reshape | solution.py:15
  41.7 1.7 fusion.47
  43.4 2.5 %fusion.29 = bf16[128,8,256]{2,0,1:T(8,128)(2,1)} fusion(bf16[8,256,256]{2,1,0:T(8,128)(2,1)S(1)} %copy-done.10, bf16[8,256,256]{2,1,0:T(8,128)(2,1)S(1)} %copy-done.12, f32[8,128,256]{2,1,0:T(8,128)S(1)} %fusion.47, bf16[16,8,8,256]{3,2,1,0:T(8,128)(2,1)} %bitcast.140), kind=kOutput, calls=%fused_computation.45 | convolution fusion | flops 270270464 | bytes 4194304 | tf_op jit(solution)/shard_map/hte,hef->thf/dot_general | solution.py:19
  45.9 1.3 copy.30
  47.2 1.0 copy.49
  48.3 117.3 %all-reduce.2.cloned.1.call-done = f32[24,65536]{1,0:T(8,128)} async-done(((f32[24,65536]{1,0:T(8,128)}), f32[24,65536]{1,0:T(8,128)}) %all-reduce.2.cloned.1.call-update) | async-done | bytes 6291472 | tf_op jit(solution)/shard_map/psum | solution.py:63
  165.5 3.6 %multiply_reduce_fusion.1 = f32[24]{0:T(128)S(1)} fusion(f32[24,65536]{1,0:T(8,128)} %all-reduce.2.cloned.1.call-done), kind=kLoop, calls=%fused_computation.13 | loop fusion | flops 3145704 | bytes 6291552 | tf_op jit(solution)/shard_map/reduce_sum | solution.py:64
  169.1 1.0 copy-done
  170.1 0.4 divide_convert_fusion.1
  170.5 0.7 copy.61
  171.3 2.7 %fusion.74 = bf16[24,256,256]{2,1,0:T(8,128)(2,1)} fusion(bf16[24,256,256]{2,1,0:T(8,128)(2,1)S(1)} %bitcast.115), kind=kOutput, calls=%fused_computation.96 | convolution fusion | flops 805306368 | bytes 6291456 | tf_op jit(solution)/shard_map/mij,mkj->mik/dot_general | solution.py:68
  173.9 7.8 %add_convert_fusion.4 = bf16[24,256,256]{2,1,0:T(8,128)(2,1)} fusion(bf16[24,256,256]{2,1,0:T(8,128)(2,1)S(1)} %bitcast.116, bf16[24,256,256]{2,1,0:T(8,128)(2,1)} %fusion.74), kind=kOutput, calls=%fused_computation.10 | convolution fusion | flops 1624768512 | bytes 9437184 | tf_op jit(solution)/shard_map/mij,mjk->mik/dot_general | solution.py:77
  181.8 5.5 %fusion.75 = bf16[24,256,256]{2,1,0:T(8,128)(2,1)} fusion(bf16[24,256,256]{2,1,0:T(8,128)(2,1)} %add_convert_fusion.4), kind=kOutput, calls=%fused_computation.97 | convolution fusion | flops 805306368 | bytes 6291456 | tf_op jit(solution)/shard_map/mij,mkj->mik/dot_general | solution.py:68
  187.3 8.2 %add_convert_fusion.2 = bf16[24,256,256]{2,1,0:T(8,128)(2,1)S(1)} fusion(bf16[24,256,256]{2,1,0:T(8,128)(2,1)} %add_convert_fusion.4, bf16[24,256,256]{2,1,0:T(8,128)(2,1)} %fusion.75), kind=kOutput, calls=%fused_computation.8 | convolution fusion | flops 1624768512 | bytes 9437184 | tf_op jit(solution)/shard_map/mij,mjk->mik/dot_general | solution.py:77
  195.5 2.7 %fusion.76 = bf16[24,256,256]{2,1,0:T(8,128)(2,1)} fusion(bf16[24,256,256]{2,1,0:T(8,128)(2,1)S(1)} %add_convert_fusion.2), kind=kOutput, calls=%fused_computation.98 | convolution fusion | flops 805306368 | bytes 6291456 | tf_op jit(solution)/shard_map/mij,mkj->mik/dot_general | solution.py:68
  198.1 11.6 %fusion.1 = (f32[24,256]{1,0:T(8,128)S(1)}, f32[24,256,256]{2,1,0:T(8,128)}) fusion(f32[3,8,256,256]{3,2,1,0:T(8,128)} %copy.45, bf16[24,256,256]{2,1,0:T(8,128)(2,1)S(1)} %add_convert_fusion.2, bf16[24,256,256]{2,1,0:T(8,128)(2,1)} %fusion.76), kind=kOutput, calls=%fused_computation.3 | convolution fusion | flops 1631053824 | bytes 18898944 | tf_op jit(solution)/shard_map/mij,mjk->mik/dot_general | solution.py:77
  209.7 6.7 %copy.44 = f32[3,8,256,256]{2,3,1,0:T(8,128)} copy(f32[3,8,256,256]{3,2,1,0:T(8,128)} %bitcast.128) | data formatting | bytes 12582912 | tf_op jit(solution)/shard_map/convert_element_type | solution.py:82
  216.5 0.0 copy-start.13
  216.5 4.6 %divide_convert_fusion = bf16[3,8,256,256]{2,3,1,0:T(8,128)(2,1)S(1)} fusion(f32[3,8,256,256]{2,3,1,0:T(8,128)} %copy.44, f32[3,8,256]{2,1,0:T(8,128)S(1)} %sqrt_bitcast_fusion, f32[3,8,256]{2,1,0:T(8,128)S(1)} %sqrt.28, bf16[1,8,256,256]{2,3,1,0:T(8,128)(2,1)S(1)} %bitcast.126, bf16[1,8,256,256]{2,3,1,0:T(8,128)(2,1)S(1)} %bitcast.123, ...), kind=kLoop, calls=%fused_computation.4 | loop fusion | flops 11010048 | bytes 12632064 | tf_op jit(solution)/shard_map/convert_element_type | solution.py:86
  221.1 1.6 copy-done.8
  222.7 0.4 fusion.31
  223.1 3.5 %convolution_convert_fusion = bf16[8,256,256]{2,1,0:T(8,128)(2,1)} fusion(f32[8,256,256]{2,1,0:T(8,128)S(1)} %fusion.31, bf16[256,8,256]{0,2,1:T(8,128)(2,1)S(1)} %bitcast.132, bf16[3,8,256,256]{2,3,1,0:T(8,128)(2,1)} %copy-done.8), kind=kOutput, calls=%fused_computation.41 | convolution fusion | flops 540540928 | bytes 6291456 | tf_op jit(solution)/shard_map/hte,hef->thf/dot_general | solution.py:19
  226.7 1.5 copy.48
  228.2 1.1 broadcast_select_fusion
  (30 shorter events, 0.1 us)
Async XLA Ops:
  7.2 1.9 copy-start.11
  7.2 3.3 %copy-start.16 = (bf16[128,2048]{1,0:T(8,128)(2,1)S(1)}, bf16[128,2048]{1,0:T(8,128)(2,1)}, u32[]{:S(2)}) copy-start(bf16[128,2048]{1,0:T(8,128)(2,1)} %param.10) | copy-start | bytes 1572868
  7.2 158.3 %all-reduce.2.cloned.1.call-start = ((), (), s32[]{:S(2)}) async-start(), calls=%async_computation | async-start | bytes 12582912 | tf_op jit(solution)/shard_map/psum | solution.py:63
  7.2 3.4 %copy-start.9 = (bf16[8,256,256]{2,1,0:T(8,128)(2,1)S(1)}, bf16[8,256,256]{2,1,0:T(8,128)(2,1)}, u32[]{:S(2)}) copy-start(bf16[8,256,256]{2,1,0:T(8,128)(2,1)} %param.15) | copy-start | bytes 3145732
  7.2 3.3 %copy-start.17 = (f32[8,128]{1,0:T(8,128)S(1)}, f32[8,128]{1,0:T(8,128)}, u32[]{:S(2)}) copy-start(f32[8,128]{1,0:T(8,128)} %param.12) | copy-start | bytes 12292
  11.1 1.0 copy-start.15
  23.4 1.2 copy-start.7
  25.1 12.5 %copy-start.1 = (bf16[8,256,256]{1,2,0:T(8,128)(2,1)}, bf16[8,256,256]{1,2,0:T(8,128)(2,1)S(1)}, u32[]{:S(2)}) copy-start(bf16[8,256,256]{1,2,0:T(8,128)(2,1)S(1)} %copy.31) | copy-start | bytes 3145732
  25.6 11.9 %copy-start.3 = (bf16[8,256,256]{1,2,0:T(8,128)(2,1)}, bf16[8,256,256]{1,2,0:T(8,128)(2,1)S(1)}, u32[]{:S(2)}) copy-start(bf16[8,256,256]{1,2,0:T(8,128)(2,1)S(1)} %copy.32) | copy-start | bytes 3145732
  27.5 10.1 %copy-start.5 = (bf16[8,256,256]{1,2,0:T(8,128)(2,1)}, bf16[8,256,256]{1,2,0:T(8,128)(2,1)S(1)}, u32[]{:S(2)}) copy-start(bf16[8,256,256]{1,2,0:T(8,128)(2,1)S(1)} %copy.33) | copy-start | bytes 3145732
  38.6 4.8 %copy-start.10 = (bf16[8,256,256]{2,1,0:T(8,128)(2,1)S(1)}, bf16[8,256,256]{2,1,0:T(8,128)(2,1)}, u32[]{:S(2)}) copy-start(bf16[8,256,256]{2,1,0:T(8,128)(2,1)} %param.15) | copy-start | bytes 3145732
  38.6 4.8 %copy-start.12 = (bf16[8,256,256]{2,1,0:T(8,128)(2,1)S(1)}, bf16[8,256,256]{2,1,0:T(8,128)(2,1)}, u32[]{:S(2)}) copy-start(bf16[8,256,256]{2,1,0:T(8,128)(2,1)} %param.14) | copy-start | bytes 3145732
  165.5 4.6 %copy-start = (f32[24,65536]{1,0:T(8,128)S(1)}, f32[24,65536]{1,0:T(8,128)}, u32[]{:S(2)}) copy-start(f32[24,65536]{1,0:T(8,128)} %all-reduce.2.cloned.1.call-done) | copy-start | bytes 18874372
  209.7 6.7 %copy-start.2 = (bf16[8,256,256]{1,2,0:T(8,128)(2,1)S(1)}, bf16[8,256,256]{1,2,0:T(8,128)(2,1)}, u32[]{:S(2)}) copy-start(bf16[8,256,256]{1,2,0:T(8,128)(2,1)} %copy-done.1) | copy-start | bytes 3145732
  209.7 6.7 %copy-start.4 = (bf16[8,256,256]{1,2,0:T(8,128)(2,1)S(1)}, bf16[8,256,256]{1,2,0:T(8,128)(2,1)}, u32[]{:S(2)}) copy-start(bf16[8,256,256]{1,2,0:T(8,128)(2,1)} %copy-done.3) | copy-start | bytes 3145732
  209.7 6.7 %copy-start.6 = (bf16[8,256,256]{1,2,0:T(8,128)(2,1)S(1)}, bf16[8,256,256]{1,2,0:T(8,128)(2,1)}, u32[]{:S(2)}) copy-start(bf16[8,256,256]{1,2,0:T(8,128)(2,1)} %copy-done.5) | copy-start | bytes 3145732
  216.5 6.2 %copy-start.13 = (bf16[256,2048]{0,1:T(8,128)(2,1)S(1)}, bf16[256,2048]{0,1:T(8,128)(2,1)}, u32[]{:S(2)}) copy-start(bf16[256,2048]{0,1:T(8,128)(2,1)} %copy.56) | copy-start | bytes 3145732
  221.1 1.6 copy-start.8
  221.1 2.1 copy-start.14
Sparse Core Ops, SparseCore 0:
  23.5 141.9 all-reduce.1
where the time goes:
time: 237 us; the launch traced here: 236 us
  waiting for transfers between devices  117 us (49%)
  matrix products  52.2 us (22%)
  local copies, waits for them, and re-layouts  34.4 us (15%)
  other arithmetic  17.2 us (7%)
  between operations  15 us (6%)
    psum x1, waiting for transfers between devices, per_device(): total = lax.psum(flat_grads, 'ctx')  117 us
    dot_general x3, matrix products, per_device(): jnp.einsum('mij,mjk->mik', polynomial, iterate, preferred_element_type=jn...  27.6 us
    unnamed x42, local copies, waits for them, and re-layouts  15.6 us
    dot_general x3, matrix products, per_device(): jnp.einsum('mij,mkj->mik', iterate, iterate, preferred_element_type=jnp.f...  10.9 us
    convert_element_type x1, local copies, waits for them, and re-layouts, per_device(): previous = jnp.stack([w_gate, w_up, w_down]).astype(jnp.float32)  6.96 us
    convert_element_type x1, local copies, waits for them, and re-layouts, per_device(): iterate.reshape(3, head_count, head_size, head_size).astype(jnp.float32)  6.7 us
    dot_general x2, matrix products, fast_apply(): jnp.einsum('hte,hef->thf', hidden, w_down, preferred_element_type=jnp.flo...  6.01 us
  transfers between devices with their start and end apart: 1, of which 1 were waited for; matrix products, arithmetic and copies ran while one was open for 10% of the time, Pallas kernels for 0%

commit v1 on v0

--- a/solution.py
+++ b/solution.py
@@ -60,7 +60,8 @@
     context_out = fast_apply(context_queries, w_gate, w_up, w_down)
     direction = directions(context_keys, context_values, token_rates, w_gate, w_up, w_down)
     flat_grads = direction.reshape(matrix_count, head_size * head_size)
-    total = lax.psum(flat_grads, "ctx")
+    h_now = lax.all_gather(flat_grads, "ctx")
+    total = jnp.sum(h_now, axis=0)
     norm_sizes = jnp.sqrt(jnp.sum(total * total, axis=1, keepdims=True))
     scaled = (total / (norm_sizes + 1e-06)).astype(jnp.bfloat16)
     iterate = scaled.reshape(matrix_count, head_size, head_size)

time: 237 us -> 623 us (2.63)
  waiting for transfers between devices: 117 us -> 467 us
  other arithmetic: 17.2 us -> 51.7 us
    all_gather x0 -> x1, waiting for transfers between devices: none -> 467 us  [per_device(): h_now = lax.all_gather(flat_grads, 'ctx')]
    psum x1 -> x0, waiting for transfers between devices: 117 us -> none  [per_device(): total = lax.psum(flat_grads, 'ctx')]
    reduce_sum x0 -> x1, other arithmetic: none -> 33.5 us  [per_device(): total = jnp.sum(h_now, axis=0)]
    another operation x0 -> x2, local copies, waits for them, and re-layouts: none -> 13.4 us  [the longest x1 6.83 us: per_device(): h_now = lax.all_gather(flat_grads, 'ctx')]
    unnamed x42 -> x39, local copies, waits for them, and re-layouts: 15.6 us -> 10.2 us
  transfers between devices with their start and end apart: 1 -> 1, of which waited for: 1 -> 1; matrix products, arithmetic and copies ran while one was open for 10% -> 3% of each run, Pallas kernels for 0% -> 0%
where the time goes in v1:
time: 623 us; the launch traced here: 622 us
  waiting for transfers between devices  467 us (75%)
  other arithmetic  51.7 us (8%)
  matrix products  50.2 us (8%)
  local copies, waits for them, and re-layouts  38.4 us (6%)
  between operations  15 us (2%)
    all_gather x1, waiting for transfers between devices, per_device(): h_now = lax.all_gather(flat_grads, 'ctx')  467 us
    reduce_sum x1, other arithmetic, per_device(): total = jnp.sum(h_now, axis=0)  33.5 us
    dot_general x3, matrix products, per_device(): jnp.einsum('mij,mjk->mik', polynomial, iterate, preferred_element_type=jn...  27.5 us
  transfers between devices with their start and end apart: 1, of which 1 were waited for; matrix products, arithmetic and copies ran while one was open for 3% of the time, Pallas kernels for 0%

profile of v1, /device:TPU:0, one launch (start us, length us, event | category | flops | bytes accessed | tf_op | source)
XLA Modules:
  0.0 622.2 jit_solution(4624900573798227612)
XLA Ops:
  7.2 0.0 copy-start.11
  7.2 0.0 all-gather.2.cloned.1.call-start
  7.2 0.0 copy-start.10
  7.3 1.8 fusion.48
  9.1 1.4 fusion.50
  10.5 0.1 convert_element_type.149
  10.6 0.5 fusion.68
  11.1 0.0 copy-start.12
  11.1 0.7 convolution_bitcast_fusion
  11.8 0.4 copy-done.12
  12.1 0.6 convolution_bitcast_fusion.2
  12.8 0.6 convolution_bitcast_fusion.1
  13.4 3.3 pad_maximum_fusion
  16.7 6.5 %copy.65 = f32[3,8,256,256]{3,2,1,0:T(8,128)} copy(f32[3,8,256,256]{2,3,1,0:T(8,128)} %pad_maximum_fusion) | data formatting | bytes 12582912 | tf_op jit(solution)/shard_map/stack | solution.py:43
  23.2 6.8 %all_gather_reshape.3 = f32[1,24,65536]{2,1,0:T(8,128)} reshape(f32[3,8,256,256]{3,2,1,0:T(8,128)} %copy.65) | data formatting | bytes 12582912 | tf_op jit(solution)/shard_map/all_gather;reshape | solution.py:63
  30.0 0.0 all-gather.2.cloned.1.call-update
  30.1 1.2 copy-done.7
  31.3 0.5 copy.53
  31.8 0.5 copy.54
  32.3 1.9 copy.55
  34.2 3.0 maximum_convert_fusion
  37.3 7.1 %copy.67 = f32[3,8,256,256]{3,2,1,0:T(8,128)} copy(f32[3,8,256,256]{2,3,1,0:T(8,128)} %maximum_convert_fusion) | data formatting | bytes 12582912 | tf_op jit(solution)/shard_map/convert_element_type | solution.py:82
  44.4 0.0 copy-start.8
  44.4 0.0 copy-start.15
  44.4 1.0 multiply_reduce_fusion
  46.1 0.3 fusion.54
  46.4 2.5 fusion.30
  48.9 0.3 copy.52
  49.2 1.0 copy.72
  50.2 466.9 %all-gather.2.cloned.1.call-done = f32[16,24,65536]{2,1,0:T(8,128)} async-done(((f32[1,24,65536]{2,1,0:T(8,128)}), f32[16,24,65536]{2,1,0:T(8,128)}) %all-gather.2.cloned.1.call-update) | async-done | bytes 100663312 | tf_op jit(solution)/shard_map/all_gather | solution.py:63
  517.1 33.5 %reduce_sum.38 = f32[24,65536]{1,0:T(8,128)} reduce(f32[16,24,65536]{2,1,0:T(8,128)} %all-gather.2.cloned.1.call-done, f32[]{:T(128)} %constant.8.clone.1), dimensions={0}, to_apply=%region_0.1 | reduce | flops 23592960 | bytes 106954752 | tf_op jit(solution)/shard_map/reduce_sum | solution.py:64
  550.6 3.6 multiply_reduce_fusion.1
  554.1 1.0 copy-done
  555.1 2.0 copy.82
  557.2 1.3 fusion
  558.5 2.7 fusion.81
  561.2 8.0 %add_convert_fusion.4 = bf16[24,256,256]{2,1,0:T(8,128)(2,1)} fusion(bf16[24,256,256]{2,1,0:T(8,128)(2,1)S(1)} %fusion, bf16[24,256,256]{2,1,0:T(8,128)(2,1)} %fusion.81), kind=kOutput, calls=%fused_computation.12 | convolution fusion | flops 1624768512 | bytes 9437184 | tf_op jit(solution)/shard_map/mij,mjk->mik/dot_general | solution.py:78
  569.3 5.5 fusion.82
  574.8 8.0 %add_convert_fusion.2 = bf16[24,256,256]{2,1,0:T(8,128)(2,1)S(1)} fusion(bf16[24,256,256]{2,1,0:T(8,128)(2,1)} %add_convert_fusion.4, bf16[24,256,256]{2,1,0:T(8,128)(2,1)} %fusion.82), kind=kOutput, calls=%fused_computation.10 | convolution fusion | flops 1624768512 | bytes 9437184 | tf_op jit(solution)/shard_map/mij,mjk->mik/dot_general | solution.py:78
  582.8 2.7 fusion.83
  585.6 11.4 %fusion.2 = (f32[24,256]{1,0:T(8,128)S(1)}, f32[24,256,256]{2,1,0:T(8,128)}) fusion(f32[3,8,256,256]{3,2,1,0:T(8,128)} %copy.67, bf16[24,256,256]{2,1,0:T(8,128)(2,1)S(1)} %add_convert_fusion.2, bf16[24,256,256]{2,1,0:T(8,128)(2,1)} %fusion.83), kind=kOutput, calls=%fused_computation.5 | convolution fusion | flops 1631053824 | bytes 18898944 | tf_op jit(solution)/shard_map/mij,mjk->mik/dot_general | solution.py:78
  597.0 6.7 %copy.66 = f32[3,8,256,256]{2,3,1,0:T(8,128)} copy(f32[3,8,256,256]{3,2,1,0:T(8,128)} %bitcast.131) | data formatting | bytes 12582912 | tf_op jit(solution)/shard_map/convert_element_type | solution.py:83
  603.7 4.8 divide_convert_fusion
  608.5 1.6 copy-done.9
  610.2 0.5 fusion.33
  610.6 2.9 convolution_convert_fusion
  613.6 0.6 copy.71
  614.2 1.1 broadcast_select_fusion
  (29 shorter events, 0.1 us)
Async XLA Ops:
  7.2 1.9 copy-start.11
  7.2 3.3 copy-start.14
  7.2 509.9 %all-gather.2.cloned.1.call-start = ((), (), s32[]{:S(2)}) async-start(), calls=%async_computation | async-start | bytes 106954752 | tf_op jit(solution)/shard_map/all_gather | solution.py:63
  7.2 3.4 copy-start.10
  7.2 3.3 copy-start.16
  11.1 1.0 copy-start.12
  30.0 1.2 copy-start.7
  31.8 12.6 %copy-start.1 = (bf16[8,256,256]{1,2,0:T(8,128)(2,1)}, bf16[8,256,256]{1,2,0:T(8,128)(2,1)S(1)}, u32[]{:S(2)}) copy-start(bf16[8,256,256]{1,2,0:T(8,128)(2,1)S(1)} %copy.53) | copy-start | bytes 3145732
  32.3 12.1 %copy-start.3 = (bf16[8,256,256]{1,2,0:T(8,128)(2,1)}, bf16[8,256,256]{1,2,0:T(8,128)(2,1)S(1)}, u32[]{:S(2)}) copy-start(bf16[8,256,256]{1,2,0:T(8,128)(2,1)S(1)} %copy.54) | copy-start | bytes 3145732
  34.2 10.2 %copy-start.5 = (bf16[8,256,256]{1,2,0:T(8,128)(2,1)}, bf16[8,256,256]{1,2,0:T(8,128)(2,1)S(1)}, u32[]{:S(2)}) copy-start(bf16[8,256,256]{1,2,0:T(8,128)(2,1)S(1)} %copy.55) | copy-start | bytes 3145732
  44.4 1.7 copy-start.8
  44.4 1.7 copy-start.15
  550.6 4.6 copy-start
  597.0 6.7 %copy-start.2 = (bf16[8,256,256]{1,2,0:T(8,128)(2,1)S(1)}, bf16[8,256,256]{1,2,0:T(8,128)(2,1)}, u32[]{:S(2)}) copy-start(bf16[8,256,256]{1,2,0:T(8,128)(2,1)} %copy-done.1) | copy-start | bytes 3145732
  597.0 6.7 %copy-start.4 = (bf16[8,256,256]{1,2,0:T(8,128)(2,1)S(1)}, bf16[8,256,256]{1,2,0:T(8,128)(2,1)}, u32[]{:S(2)}) copy-start(bf16[8,256,256]{1,2,0:T(8,128)(2,1)} %copy-done.3) | copy-start | bytes 3145732
  597.0 6.7 %copy-start.6 = (bf16[8,256,256]{1,2,0:T(8,128)(2,1)S(1)}, bf16[8,256,256]{1,2,0:T(8,128)(2,1)}, u32[]{:S(2)}) copy-start(bf16[8,256,256]{1,2,0:T(8,128)(2,1)} %copy-done.5) | copy-start | bytes 3145732
  603.7 6.4 %copy-start.13 = (bf16[256,2048]{1,0:T(8,128)(2,1)S(1)}, bf16[256,2048]{1,0:T(8,128)(2,1)}, u32[]{:S(2)}) copy-start(bf16[256,2048]{1,0:T(8,128)(2,1)} %param.16) | copy-start | bytes 3145732
  608.5 1.6 copy-start.9
Sparse Core Ops, SparseCore 0:
  30.2 486.8 all-gather.1
